TPU v7x, 32 devices: a whole 2x2x4 slice. The times are simulated.
32 devices in a mesh: fsdp: 4 (over y, core), ctx: 4 (over z), uly: 2 (over x).
Axes of the slice: x: 2, y: 2, z: 4, core: 2. Of those that a mesh axis runs over, the one named last changes fastest.
Arguments:
- query_states: bfloat16 [12, 384, 8192], P('fsdp', 'ctx', 'uly'), may hold values from -8 to 8
- key_projections: bfloat16 [12, 384, 1024], P('fsdp', 'ctx', 'uly'), may hold values from -8 to 8
- value_projections: bfloat16 [12, 384, 1024], P('fsdp', 'ctx', 'uly'), may hold values from -6 to 6
- layer_bias: bfloat16 [10240], P('fsdp'), may hold values from -3 to 3
- positions: int32 [12, 384], P('fsdp', 'ctx'), may hold values from 0 to 383, as said below
- rescale: float32 [2, 64], replicated, may hold values from 1 to 16
- table_index: int32 [12], P('fsdp'), may hold values from 0 to 1
Outputs:
- attended: bfloat16 [12, 384, 8192], P('fsdp', 'ctx', 'uly')
Inputs may be any that keep to these rules, and one draw needn't show every extreme that they name: In each sequence the rows come in aligned runs of 48; every run holds 48 consecutive positions in increasing order, starting at a multiple of 48, and every position 0 to 383 occurs once. The order of the runs differs between sequences.
All inputs are finite; a program needn't handle non-finite values.
Results may differ from a plain program's by a relative error of at most 0.012.
Values may be sent and summed in bfloat16 or wider, within the bound.
A program may use at most 64 MiB of HBM per device.

v0:
```python
import math
import jax
import jax.numpy as jnp
from jax import lax
from jax.sharding import PartitionSpec as P

QUERY_HEADS = 64
KEY_VALUE_HEADS = 8
HEAD_SIZE = 128
rope_base = 1000000.0
masked_value = -1e30


def apply_rotation(states, positions, scale_factors):
    half_dim = states.shape[-1] // 2
    exponent = jnp.arange(half_dim, dtype=jnp.float32) * (2.0 / states.shape[-1])
    inverse = 1.0 / (scale_factors * jnp.power(jnp.float32(rope_base), exponent)[None, :])
    angles = positions.astype(jnp.float32)[:, :, None] * inverse[:, None, :]
    cosine = jnp.cos(angles)[:, :, None, :]
    sine_wave = jnp.sin(angles)[:, :, None, :]
    leading = states[..., :half_dim]
    trailing = states[..., half_dim:]
    return jnp.concatenate(
        [leading * cosine - trailing * sine_wave, trailing * cosine + leading * sine_wave], axis=-1
    )


def make_folder(query_grouped, query_positions, key_heads_here):

    def attend(running, block_piece):
        highest, totals, weighted_blend = running
        block_keys, block_values, block_positions = block_piece
        key_rows = block_keys.reshape(-1, key_heads_here, HEAD_SIZE)
        value_rows = block_values.reshape(-1, key_heads_here, HEAD_SIZE)
        scores = jnp.einsum(
            "qgrd,kgd->grqk", query_grouped, key_rows, preferred_element_type=jnp.float32
        ) / math.sqrt(HEAD_SIZE)
        allowed = block_positions[0][None, :] <= query_positions[0][:, None]
        block_high = jnp.max(jnp.where(allowed, scores, masked_value), axis=-1)
        new_high = jnp.maximum(highest, block_high)
        weights = jnp.where(allowed, jnp.exp(scores - new_high[..., None]), 0.0)
        shrink = jnp.exp(highest - new_high)
        totals = jnp.sum(weights, axis=-1)
        weighted_blend = jnp.einsum(
            "grqk,kgd->grqd",
            weights.astype(jnp.bfloat16),
            value_rows,
            preferred_element_type=jnp.float32,
        )
        return (new_high, totals, weighted_blend)

    def folder(running, block_piece, offset):
        return attend(running, block_piece)

    return folder


def initial_state(key_heads_here, group_fraction, query_rows):
    return (
        jnp.full((key_heads_here, group_fraction, query_rows), masked_value, jnp.float32),
        jnp.zeros((key_heads_here, group_fraction, query_rows), jnp.float32),
        jnp.zeros((key_heads_here, group_fraction, query_rows, HEAD_SIZE), jnp.float32),
    )


def finish(running, query_rows):
    highest, totals, weighted_blend = running
    normalized = weighted_blend / totals[..., None]
    return normalized.transpose(2, 0, 1, 3).reshape(1, query_rows, -1).astype(jnp.bfloat16)


def on_device(
    query_states, key_projections, value_projections, layer_bias, positions, rescale, table_index
):
    bias_terms = lax.all_gather(layer_bias, "fsdp", axis=0, tiled=True).astype(jnp.float32)
    local_count = query_states.shape[0]
    tokens_here = query_states.shape[1]
    query_heads_here = query_states.shape[2] // HEAD_SIZE
    key_heads_here = key_projections.shape[2] // HEAD_SIZE
    uly_place = lax.axis_index("uly")
    query_span_width = QUERY_HEADS * HEAD_SIZE
    key_span_width = KEY_VALUE_HEADS * HEAD_SIZE
    query_bias = lax.dynamic_slice_in_dim(
        bias_terms[:query_span_width].reshape(QUERY_HEADS, HEAD_SIZE),
        uly_place * query_heads_here,
        query_heads_here,
        0,
    )
    key_offset_bias = lax.dynamic_slice_in_dim(
        bias_terms[query_span_width : query_span_width + key_span_width].reshape(
            KEY_VALUE_HEADS, HEAD_SIZE
        ),
        uly_place * key_heads_here,
        key_heads_here,
        0,
    )
    value_offset_bias = lax.dynamic_slice_in_dim(
        bias_terms[query_span_width + key_span_width :].reshape(KEY_VALUE_HEADS, HEAD_SIZE),
        uly_place * key_heads_here,
        key_heads_here,
        0,
    )
    selector = (
        jnp.arange(rescale.shape[0], dtype=jnp.int32)[None, :] == table_index[:, None]
    ).astype(jnp.float32)
    scale_factors = jnp.dot(selector, rescale, precision=lax.Precision.HIGHEST)
    query_rotated_all = apply_rotation(
        query_states.astype(jnp.float32).reshape(
            local_count, tokens_here, query_heads_here, HEAD_SIZE
        )
        + query_bias,
        positions,
        scale_factors,
    )
    query_rotated_all = query_rotated_all.astype(jnp.bfloat16).reshape(
        local_count, tokens_here, query_heads_here * HEAD_SIZE
    )
    key_rotated_all = apply_rotation(
        key_projections.astype(jnp.float32).reshape(
            local_count, tokens_here, key_heads_here, HEAD_SIZE
        )
        + key_offset_bias,
        positions,
        scale_factors,
    )
    key_rotated_all = key_rotated_all.astype(jnp.bfloat16).reshape(
        local_count, tokens_here, key_heads_here * HEAD_SIZE
    )
    value_all = (
        value_projections.astype(jnp.float32).reshape(
            local_count, tokens_here, key_heads_here, HEAD_SIZE
        )
        + value_offset_bias
    ).astype(jnp.bfloat16)
    value_all = value_all.reshape(local_count, tokens_here, key_heads_here * HEAD_SIZE)
    group_fraction = QUERY_HEADS // KEY_VALUE_HEADS
    results = []
    for member in range(local_count):
        query_rotated_rows = query_rotated_all[member : member + 1]
        key_rotated_rows = key_rotated_all[member : member + 1]
        value_with_bias = value_all[member : member + 1]
        member_positions = positions[member : member + 1]
        query_grouped = query_rotated_rows.reshape(
            tokens_here, key_heads_here, group_fraction, HEAD_SIZE
        )
        folder = make_folder(query_grouped, member_positions, key_heads_here)
        running = folder(
            initial_state(key_heads_here, group_fraction, tokens_here),
            (
                lax.all_gather(key_rotated_rows, "ctx", axis=1, tiled=True),
                lax.all_gather(value_with_bias, "ctx", axis=1, tiled=True),
                lax.all_gather(member_positions, "ctx", axis=1, tiled=True),
            ),
            jnp.int32(0),
        )
        results.append(finish(running, tokens_here))
    return jnp.concatenate(results, axis=0)


def solution(mesh):
    in_specs = (
        P("fsdp", "ctx", "uly"),
        P("fsdp", "ctx", "uly"),
        P("fsdp", "ctx", "uly"),
        P("fsdp"),
        P("fsdp", "ctx"),
        P(),
        P("fsdp"),
    )
    out_specs = P("fsdp", "ctx", "uly")
    return jax.shard_map(
        on_device, mesh=mesh, in_specs=in_specs, out_specs=out_specs, check_vma=False
    )
```

profile of v0, /device:TPU:0, one launch (start us, length us, event | category | flops | bytes accessed | tf_op | source)
XLA Modules:
  0.0 148.7 jit_solution(562633976710418100)
XLA Ops:
  0.0 0.8 reshape.188
  0.9 6.2 %all-gather = bf16[4,1,2560]{2,1,0:T(2,128)(2,1)S(1)} all-gather(bf16[1,1,2560]{2,1,0:T(2,128)(2,1)S(1)} %reshape.188), channel_id=1, replica_groups=mesh['fsdp'=4,'ctx'=4,'uly'=2] {'fsdp'}, dimensions={0}, use_global_device_ids=true | all-gather | bytes 25600 | tf_op jit(solution)/shard_map/all_gather | solution.py:75
  7.1 0.7 convert_element_type.79
  7.7 0.7 slice_bitcast_fusion.2
  8.4 1.1 reshape.174
  9.6 0.8 fusion.42
  10.5 0.7 convert_element_type.68
  11.2 0.6 multiply_cosine_fusion
  11.8 0.6 subtract_convert_fusion.1
  12.3 1.0 fusion.46
  13.4 15.4 %all_gather.32 = bf16[1,384,512]{2,1,0:T(8,128)(2,1)S(1)} all-gather(bf16[1,96,512]{2,1,0:T(8,128)(2,1)S(1)} %slice.114), channel_id=1, replica_groups=mesh['fsdp'=4,'ctx'=4,'uly'=2] {'ctx'}, dimensions={1}, use_global_device_ids=true | all-gather | bytes 491520 | tf_op jit(solution)/shard_map/all_gather | solution.py:150
  28.8 0.2 copy.23
  29.0 0.8 slice_bitcast_fusion
  29.8 0.6 bitcast_add_fusion
  30.4 1.7 %subtract_convert_fusion = (bf16[3,96,32,64]{3,1,2,0:T(8,128)(2,1)S(1)}, bf16[3,96,32,64]{3,1,2,0:T(8,128)(2,1)S(1)}) fusion(f32[3,96,32,128]{3,1,2,0:T(8,128)S(1)} %bitcast_add_fusion, f32[3,96,64]{2,1,0:T(8,128)S(1)} %get-tuple-element.24, f32[3,96,64]{2,1,0:T(8,128)S(1)} %get-tuple-element.23), kind=kLoop, calls=%fused_computation.18 | loop fusion | flops 4718592 | bytes 7225344 | tf_op jit(solution)/shard_map/convert.3
  32.1 1.3 fusion.44
  33.4 0.6 dynamic-slice
  35.0 9.2 %all-reduce.3 = (s32[384]{0:T(512)}, s32[384]{0:T(512)}, s32[384]{0:T(512)S(1)}) all-reduce(s32[384]{0:T(512)S(1)} %fusion.56, s32[384]{0:T(512)S(1)} %fusion.55, s32[384]{0:T(512)S(1)} %fusion.54), channel_id=1, replica_groups=mesh['fsdp'=4,'ctx'=4,'uly'=2] {'ctx'}, use_global_device_ids=true, to_apply=%add.2 | all-reduce | flops 1152 | bytes 9216
  44.3 1.0 fusion.6
  45.3 2.1 %copy-done.1 = f32[4,384,96,8]{1,2,3,0:T(8,128)} copy-done((f32[4,384,96,8]{1,2,3,0:T(8,128)}, f32[4,384,96,8]{1,2,3,0:T(8,128)S(1)}, u32[]{:S(2)}) %copy-start.1) | copy-done | bytes 4718616
  47.5 1.6 %fusion.9 = f32[4,8,96]{2,1,0:T(8,128)S(1)} fusion(f32[4,384,96,8]{1,2,3,0:T(8,128)S(1)} %get-tuple-element.33, f32[4,8,96]{2,1,0:T(8,128)S(1)} %broadcast_maximum_fusion.2, pred[96,384]{1,0:T(8,128)(4,1)S(1)} %broadcast_compare_fusion.2), kind=kLoop, calls=%fused_computation.19 | loop fusion | flops 4715520 | bytes 4780032 | tf_op jit(solution)/shard_map/reduce_sum | solution.py:43
  49.1 0.2 reshape.178
  49.5 15.1 %all_gather.33 = bf16[1,384,512]{2,1,0:T(8,128)(2,1)S(1)} all-gather(bf16[1,96,512]{2,1,0:T(8,128)(2,1)S(1)} %slice.123), channel_id=1, replica_groups=mesh['fsdp'=4,'ctx'=4,'uly'=2] {'ctx'}, dimensions={1}, use_global_device_ids=true | all-gather | bytes 491520 | tf_op jit(solution)/shard_map/all_gather | solution.py:151
  64.6 0.2 copy.26
  64.9 3.7 %fusion.35 = bf16[96,4,8,128]{3,0,2,1:T(8,128)(2,1)S(1)} fusion(bf16[384,4,128,1]{0,2,3,1:T(8,128)(2,1)S(1)} %bitcast.148, f32[4,384,96,8]{1,2,3,0:T(8,128)} %copy-done.1, f32[4,8,96]{2,1,0:T(8,128)S(1)} %broadcast_maximum_fusion.2, pred[96,384]{1,0:T(8,128)(4,1)S(1)} %broadcast_compare_fusion.2, f32[96,4,8]{0,2,1:T(8,128)S(1)} %bitcast.151), kind=kOutput, calls=%fused_computation.50 | convolution fusion | flops 307494912 | bytes 5959680 | tf_op jit(solution)/shard_map/grqk,kgd->grqd/dot_general | solution.py:44
  68.6 0.3 copy.28
  68.9 0.3 convert_element_type.72
  69.3 14.4 %all_gather.35 = bf16[1,384,512]{2,1,0:T(8,128)(2,1)S(1)} all-gather(bf16[1,96,512]{2,1,0:T(8,128)(2,1)S(1)} %slice.126), channel_id=1, replica_groups=mesh['fsdp'=4,'ctx'=4,'uly'=2] {'ctx'}, dimensions={1}, use_global_device_ids=true | all-gather | bytes 491520 | tf_op jit(solution)/shard_map/all_gather | solution.py:150
  83.7 0.2 copy.29
  84.1 1.0 fusion.3
  85.1 2.1 %copy-done.3 = f32[4,384,96,8]{1,2,3,0:T(8,128)} copy-done((f32[4,384,96,8]{1,2,3,0:T(8,128)}, f32[4,384,96,8]{1,2,3,0:T(8,128)S(1)}, u32[]{:S(2)}) %copy-start.3) | copy-done | bytes 4718616
  87.2 1.6 %fusion.11 = f32[4,8,96]{2,1,0:T(8,128)S(1)} fusion(f32[4,384,96,8]{1,2,3,0:T(8,128)S(1)} %get-tuple-element.31, f32[4,8,96]{2,1,0:T(8,128)S(1)} %broadcast_maximum_fusion.1, pred[96,384]{1,0:T(8,128)(4,1)S(1)} %broadcast_compare_fusion.1), kind=kLoop, calls=%fused_computation.21 | loop fusion | flops 4715520 | bytes 4780032 | tf_op jit(solution)/shard_map/reduce_sum | solution.py:43
  88.9 14.4 %all_gather.36 = bf16[1,384,512]{2,1,0:T(8,128)(2,1)S(1)} all-gather(bf16[1,96,512]{2,1,0:T(8,128)(2,1)S(1)} %slice.129), channel_id=1, replica_groups=mesh['fsdp'=4,'ctx'=4,'uly'=2] {'ctx'}, dimensions={1}, use_global_device_ids=true | all-gather | bytes 491520 | tf_op jit(solution)/shard_map/all_gather | solution.py:151
  103.3 0.2 copy.31
  103.5 3.7 %fusion.34 = bf16[96,4,8,128]{3,0,2,1:T(8,128)(2,1)S(1)} fusion(bf16[384,4,128,1]{0,2,3,1:T(8,128)(2,1)S(1)} %bitcast.149, f32[4,384,96,8]{1,2,3,0:T(8,128)} %copy-done.3, f32[4,8,96]{2,1,0:T(8,128)S(1)} %broadcast_maximum_fusion.1, pred[96,384]{1,0:T(8,128)(4,1)S(1)} %broadcast_compare_fusion.1, f32[96,4,8]{0,2,1:T(8,128)S(1)} %bitcast.153), kind=kOutput, calls=%fused_computation.48 | convolution fusion | flops 307494912 | bytes 5959680 | tf_op jit(solution)/shard_map/grqk,kgd->grqd/dot_general | solution.py:44
  107.2 0.3 copy.33
  107.5 0.3 convert_element_type.75
  107.9 15.1 %all_gather.38 = bf16[1,384,512]{2,1,0:T(8,128)(2,1)S(1)} all-gather(bf16[1,96,512]{2,1,0:T(8,128)(2,1)S(1)} %slice.132), channel_id=1, replica_groups=mesh['fsdp'=4,'ctx'=4,'uly'=2] {'ctx'}, dimensions={1}, use_global_device_ids=true | all-gather | bytes 491520 | tf_op jit(solution)/shard_map/all_gather | solution.py:150
  123.0 0.2 copy.34
  123.4 1.0 fusion
  124.4 2.1 %copy-done.2 = f32[4,384,96,8]{1,2,3,0:T(8,128)} copy-done((f32[4,384,96,8]{1,2,3,0:T(8,128)}, f32[4,384,96,8]{1,2,3,0:T(8,128)S(1)}, u32[]{:S(2)}) %copy-start.2) | copy-done | bytes 4718616
  126.5 1.6 %fusion.13 = f32[4,8,96]{2,1,0:T(8,128)S(1)} fusion(f32[4,384,96,8]{1,2,3,0:T(8,128)S(1)} %get-tuple-element.29, f32[4,8,96]{2,1,0:T(8,128)S(1)} %broadcast_maximum_fusion, pred[96,384]{1,0:T(8,128)(4,1)S(1)} %broadcast_compare_fusion), kind=kLoop, calls=%fused_computation.23 | loop fusion | flops 4715520 | bytes 4780032 | tf_op jit(solution)/shard_map/reduce_sum | solution.py:43
  128.2 14.3 %all_gather.39 = bf16[1,384,512]{2,1,0:T(8,128)(2,1)S(1)} all-gather(bf16[1,96,512]{2,1,0:T(8,128)(2,1)S(1)} %slice.135), channel_id=1, replica_groups=mesh['fsdp'=4,'ctx'=4,'uly'=2] {'ctx'}, dimensions={1}, use_global_device_ids=true | all-gather | bytes 491520 | tf_op jit(solution)/shard_map/all_gather | solution.py:151
  142.4 0.2 copy.36
  142.7 3.7 %fusion.33 = bf16[96,4,8,128]{3,0,2,1:T(8,128)(2,1)S(1)} fusion(bf16[384,4,128,1]{0,2,3,1:T(8,128)(2,1)S(1)} %bitcast.150, f32[4,384,96,8]{1,2,3,0:T(8,128)} %copy-done.2, f32[4,8,96]{2,1,0:T(8,128)S(1)} %broadcast_maximum_fusion, pred[96,384]{1,0:T(8,128)(4,1)S(1)} %broadcast_compare_fusion, f32[96,4,8]{0,2,1:T(8,128)S(1)} %bitcast.152), kind=kOutput, calls=%fused_computation.46 | convolution fusion | flops 307494912 | bytes 5959680 | tf_op jit(solution)/shard_map/grqk,kgd->grqd/dot_general | solution.py:44
  146.4 0.3 copy.38
  146.7 0.3 convert_element_type.78
  147.0 1.7 %pad_maximum_fusion = bf16[3,96,4096]{2,1,0:T(8,128)(2,1)} fusion(bf16[1,96,4096]{2,1,0:T(8,128)(2,1)S(1)} %convert_element_type.78, bf16[1,96,4096]{2,1,0:T(8,128)(2,1)S(1)} %convert_element_type.75, bf16[1,96,4096]{2,1,0:T(8,128)(2,1)S(1)} %convert_element_type.72), kind=kLoop, calls=%fused_computation.28 | loop fusion | flops 2359296 | bytes 4718592 | tf_op jit(solution)/shard_map/concatenate | solution.py:157
  (45 shorter events, 1.2 us)
Async XLA Ops:
  0.0 9.6 %copy-start = (f32[2,64]{1,0:T(2,128)S(1)}, f32[2,64]{1,0:T(2,128)}, u32[]{:S(2)}) copy-start(f32[2,64]{1,0:T(2,128)} %param.12) | copy-start | bytes 1540
  0.0 29.8 %copy-start.4 = (bf16[3,96,4096]{2,1,0:T(8,128)(2,1)S(1)}, bf16[3,96,4096]{2,1,0:T(8,128)(2,1)}, u32[]{:S(2)}) copy-start(bf16[3,96,4096]{2,1,0:T(8,128)(2,1)} %param.7) | copy-start | bytes 7077892
  32.1 1.3 copy-start.10
  32.1 2.6 %copy-start.7 = (s32[3,96]{1,0:T(4,128)S(1)}, s32[3,96]{1,0:T(4,128)}, u32[]{:S(2)}) copy-start(s32[3,96]{1,0:T(4,128)} %param.11) | copy-start | bytes 3460
  44.3 4.8 %copy-start.6 = (bf16[3,96,512]{2,1,0:T(8,128)(2,1)S(1)}, bf16[3,96,512]{2,1,0:T(8,128)(2,1)}, u32[]{:S(2)}) copy-start(bf16[3,96,512]{2,1,0:T(8,128)(2,1)} %param.9) | copy-start | bytes 884740
  45.3 2.1 %copy-start.1 = (f32[4,384,96,8]{1,2,3,0:T(8,128)}, f32[4,384,96,8]{1,2,3,0:T(8,128)S(1)}, u32[]{:S(2)}) copy-start(f32[4,384,96,8]{1,2,3,0:T(8,128)S(1)} %get-tuple-element.33) | copy-start | bytes 14155780
  64.9 4.4 %copy-start.5 = (bf16[1,96,4,128]{3,2,1,0:T(4,128)(2,1)S(1)}, bf16[1,96,4,128]{3,2,1,0:T(4,128)(2,1)}, u32[]{:S(2)}) copy-start(bf16[1,96,4,128]{3,2,1,0:T(4,128)(2,1)} %get-tuple-element.17) | copy-start | bytes 294916
  64.9 19.1 %copy-start.9 = (s32[384]{0:T(512)S(1)}, s32[384]{0:T(512)}, u32[]{:S(2)}) copy-start(s32[384]{0:T(512)} %get-tuple-element.6) | copy-start | bytes 4612
  85.1 2.1 %copy-start.3 = (f32[4,384,96,8]{1,2,3,0:T(8,128)}, f32[4,384,96,8]{1,2,3,0:T(8,128)S(1)}, u32[]{:S(2)}) copy-start(f32[4,384,96,8]{1,2,3,0:T(8,128)S(1)} %get-tuple-element.31) | copy-start | bytes 14155780
  103.5 19.7 %copy-start.8 = (s32[384]{0:T(512)S(1)}, s32[384]{0:T(512)}, u32[]{:S(2)}) copy-start(s32[384]{0:T(512)} %get-tuple-element.5) | copy-start | bytes 4612
  124.4 2.1 %copy-start.2 = (f32[4,384,96,8]{1,2,3,0:T(8,128)}, f32[4,384,96,8]{1,2,3,0:T(8,128)S(1)}, u32[]{:S(2)}) copy-start(f32[4,384,96,8]{1,2,3,0:T(8,128)S(1)} %get-tuple-element.29) | copy-start | bytes 14155780
where the time goes:
time: 149 us
  blocking collectives  104 us (70%)
  matrix products  15.1 us (10%)
  local copies, waits for them, and re-layouts  14.5 us (10%)
  other arithmetic  14 us (9%)
    all_gather x3, blocking collectives, on_device(): lax.all_gather(key_rotated_rows, 'ctx', axis=1, tiled=True)  44.9 us
    all_gather x3, blocking collectives, on_device(): lax.all_gather(value_with_bias, 'ctx', axis=1, tiled=True)  43.8 us
    dot_general x3, matrix products, attend(): jnp.einsum('grqk,kgd->grqd', weights.astype(jnp.bfloat16), value_rows, pr...  11.1 us
    unnamed x1, blocking collectives  9.2 us
    unnamed x32, local copies, waits for them, and re-layouts  8.12 us
    all_gather x1, blocking collectives, on_device(): lax.all_gather(layer_bias, 'fsdp', axis=0, tiled=True).astype(jnp.float32)  6.2 us
    reduce_sum x3, other arithmetic, attend(): totals = jnp.sum(weights, axis=-1)  4.82 us
    dot_general x3, matrix products, attend(): jnp.einsum('qgrd,kgd->grqk', query_grouped, key_rows, preferred_element_t...  3.1 us

commit v1 on v0

--- a/solution.py
+++ b/solution.py
@@ -9,6 +9,22 @@
 HEAD_SIZE = 128
 rope_base = 1000000.0
 masked_value = -1e30
+
+
+def gather_around(x, axis, dim):
+    ways, here, turn = (lax.axis_size(axis), lax.axis_index(axis), x.shape[dim])
+    lengths = [n * ways if d == dim else n for d, n in enumerate(x.shape)]
+    full = lax.dynamic_update_slice_in_dim(jnp.zeros(lengths, x.dtype), x, here * turn, axis=dim)
+    going_up = going_down = x
+    for far in range(1, ways // 2 + 1):
+        going_up = lax.ppermute(going_up, axis, [(d, (d + 1) % ways) for d in range(ways)])
+        full = lax.dynamic_update_slice_in_dim(full, going_up, (here - far) % ways * turn, axis=dim)
+        if 2 * far < ways:
+            going_down = lax.ppermute(going_down, axis, [(d, (d - 1) % ways) for d in range(ways)])
+            full = lax.dynamic_update_slice_in_dim(
+                full, going_down, (here + far) % ways * turn, axis=dim
+            )
+    return full
 
 
 def apply_rotation(states, positions, scale_factors):
@@ -148,7 +164,7 @@
             initial_state(key_heads_here, group_fraction, tokens_here),
             (
                 lax.all_gather(key_rotated_rows, "ctx", axis=1, tiled=True),
-                lax.all_gather(value_with_bias, "ctx", axis=1, tiled=True),
+                gather_around(value_with_bias, "ctx", 1),
                 lax.all_gather(member_positions, "ctx", axis=1, tiled=True),
             ),
             jnp.int32(0),

time: 149 us -> 141 us (0.946)
  blocking collectives: 104 us -> 59.6 us
  starting transfers between devices: 0 us -> 12.6 us
  local copies, waits for them, and re-layouts: 14.5 us -> 26.1 us
  other arithmetic: 14 us -> 21.2 us
  matrix products: 15.1 us -> 19.6 us
    all_gather x3 -> x0, blocking collectives: 43.8 us -> none  [on_device(): lax.all_gather(value_with_bias, 'ctx', axis=1, tiled=True)]
    dynamic_update_slice x0 -> x12, local copies, waits for them, and re-layouts: none -> 16.3 us  [the longest x6 8.31 us: gather_around(): lax.dynamic_update_slice_in_dim(full, going_up, (here - far) % ways * tur...]
    ppermute x0 -> x9, starting transfers between devices: none -> 12.6 us  [the longest x3 7.4 us: gather_around(): lax.ppermute(going_down, axis, [(d, (d - 1) % ways) for d in range(ways)])]
    dot_general x3, matrix products: 3.1 us -> 8.37 us  [attend(): jnp.einsum('qgrd,kgd->grqk', query_grouped, key_rows, preferred_element_t...]
    unnamed x32 -> x44, local copies, waits for them, and re-layouts: 8.12 us -> 3.95 us
    concatenate x2, other arithmetic: 2.32 us -> 5.17 us  [apply_rotation(): jnp.concatenate([leading * cosine - trailing * sine_wave, trailing * cosi...]
    reduce_sum x3, other arithmetic: 4.82 us -> 7.15 us  [attend(): totals = jnp.sum(weights, axis=-1)]
    another operation x2, other arithmetic: 2.26 us -> 4.13 us
  transfers between devices with their start and end apart: 0 -> 9, of which waited for: 0 -> 0; matrix products, arithmetic and copies ran while one was open for 0% -> 40% of each run, Pallas kernels for 0% -> 0%
where the time goes in v1:
time: 141 us; the launch traced here: 140 us
  blocking collectives  59.6 us (42%)
  local copies, waits for them, and re-layouts  26.1 us (19%)
  other arithmetic  21.2 us (15%)
  matrix products  19.6 us (14%)
  starting transfers between devices  12.6 us (9%)
    all_gather x3, blocking collectives, on_device(): lax.all_gather(key_rotated_rows, 'ctx', axis=1, tiled=True)  44.8 us
    dot_general x3, matrix products, attend(): jnp.einsum('grqk,kgd->grqd', weights.astype(jnp.bfloat16), value_rows, pr...  11.1 us
    unnamed x1, blocking collectives  8.52 us
    dot_general x3, matrix products, attend(): jnp.einsum('qgrd,kgd->grqk', query_grouped, key_rows, preferred_element_t...  8.37 us
    dynamic_update_slice x6, local copies, waits for them, and re-layouts, gather_around(): lax.dynamic_update_slice_in_dim(full, going_up, (here - far) % ways * tur...  8.31 us
    ppermute x3, starting transfers between devices, gather_around(): lax.ppermute(going_down, axis, [(d, (d - 1) % ways) for d in range(ways)])  7.4 us
    reduce_sum x3, other arithmetic, attend(): totals = jnp.sum(weights, axis=-1)  7.15 us
    all_gather x1, blocking collectives, on_device(): lax.all_gather(layer_bias, 'fsdp', axis=0, tiled=True).astype(jnp.float32)  6.2 us
  transfers between devices with their start and end apart: 9, of which 0 were waited for; matrix products, arithmetic and copies ran while one was open for 40% of the time, Pallas kernels for 0%

profile of v1, /device:TPU:0, one launch (start us, length us, event | category | flops | bytes accessed | tf_op | source)
XLA Modules:
  0.0 140.4 jit_solution(15576002643564716948)
XLA Ops:
  0.0 0.7 reshape.188
  0.7 6.2 %all-gather = bf16[4,1,2560]{2,1,0:T(2,128)(2,1)S(1)} all-gather(bf16[1,1,2560]{2,1,0:T(2,128)(2,1)S(1)} %reshape.188), channel_id=1, replica_groups=mesh['fsdp'=4,'ctx'=4,'uly'=2] {'fsdp'}, dimensions={0}, use_global_device_ids=true | all-gather | bytes 25600 | tf_op jit(solution)/shard_map/all_gather | solution.py:91
  7.0 1.1 copy.45
  8.3 0.8 fusion.57
  9.1 2.0 %collective-permute-start = (bf16[1,96,512]{1,2,0:T(8,128)(2,1)}, bf16[1,96,512]{1,2,0:T(8,128)(2,1)}, u32[]{:S(2)}, u32[]{:S(2)}) collective-permute-start(bf16[1,96,512]{1,2,0:T(8,128)(2,1)} %bitcast.11), channel_id=1, source_target_pairs={{0,2},{2,4},{4,6},{6,0},{1,3},{3,5},{5,7},{7,1},{8,10},{10,12},{12... | collective-permute-start | bytes 294920 | tf_op jit(solution)/shard_map/ppermute | solution.py:20
  11.1 2.0 %collective-permute-start.1 = (bf16[1,96,512]{1,2,0:T(8,128)(2,1)}, bf16[1,96,512]{1,2,0:T(8,128)(2,1)}, u32[]{:S(2)}, u32[]{:S(2)}) collective-permute-start(bf16[1,96,512]{1,2,0:T(8,128)(2,1)} %bitcast.11), channel_id=1, source_target_pairs={{0,6},{2,0},{4,2},{6,4},{1,7},{3,1},{5,3},{7,5},{8,14},{10,8},{12,... | collective-permute-start | bytes 294920 | tf_op jit(solution)/shard_map/ppermute | solution.py:23
  13.2 3.8 %collective-permute-start.4 = (bf16[1,96,512]{1,2,0:T(8,128)(2,1)}, bf16[1,96,512]{1,2,0:T(8,128)(2,1)}, u32[]{:S(2)}, u32[]{:S(2)}) collective-permute-start(bf16[1,96,512]{1,2,0:T(8,128)(2,1)} %bitcast.21), channel_id=1, source_target_pairs={{0,6},{2,0},{4,2},{6,4},{1,7},{3,1},{5,3},{7,5},{8,14},{10,8},{12,... | collective-permute-start | bytes 294920 | tf_op jit(solution)/shard_map/ppermute | solution.py:23
  17.0 0.7 convert_element_type.68
  17.7 1.4 slice_bitcast_fusion.5
  19.1 1.1 reshape.174
  20.5 0.6 multiply_cosine_fusion
  21.1 0.5 subtract_convert_fusion.1
  21.8 1.1 fusion.46
  22.9 15.0 %all_gather.23 = bf16[1,384,512]{2,1,0:T(8,128)(2,1)S(1)} all-gather(bf16[1,96,512]{2,1,0:T(8,128)(2,1)S(1)} %slice.114), channel_id=1, replica_groups=mesh['fsdp'=4,'ctx'=4,'uly'=2] {'ctx'}, dimensions={1}, use_global_device_ids=true | all-gather | bytes 491520 | tf_op jit(solution)/shard_map/all_gather | solution.py:166
  38.2 0.6 bitcast_add_fusion
  39.1 3.6 %subtract_convert_fusion = (bf16[3,96,32,64]{3,1,2,0:T(8,128)(2,1)S(1)}, bf16[3,96,32,64]{3,1,2,0:T(8,128)(2,1)}) fusion(f32[3,96,32,128]{3,1,2,0:T(8,128)S(1)} %bitcast_add_fusion, f32[3,96,64]{2,1,0:T(8,128)S(1)} %copy-done.7, f32[3,96,64]{2,1,0:T(8,128)} %copy-done.5), kind=kLoop, calls=%fused_computation.18 | loop fusion | flops 4718592 | bytes 7225344 | tf_op jit(solution)/shard_map/convert.3
  42.7 0.7 dynamic-slice
  44.4 4.1 %fusion.44 = (bf16[1,96,32,128]{3,1,2,0:T(8,128)(2,1)}, bf16[1,96,32,128]{3,1,2,0:T(8,128)(2,1)S(1)}, bf16[1,96,32,128]{3,1,2,0:T(8,128)(2,1)}) fusion(bf16[3,96,32,64]{3,1,2,0:T(8,128)(2,1)S(1)} %get-tuple-element.8, bf16[3,96,32,64]{3,1,2,0:T(8,128)(2,1)} %get-tuple-element.9), kind=kLoop, calls=%fused_computation.54 | loop fusion | flops 4718592 | bytes 4718592 | tf_op jit(solution)/shard_map/concatenate | solution.py:39
  48.5 8.5 %all-reduce.3 = (s32[384]{0:T(512)S(1)}, s32[384]{0:T(512)S(1)}, s32[384]{0:T(512)S(1)}) all-reduce(s32[384]{0:T(512)S(1)} %fusion.56, s32[384]{0:T(512)S(1)} %fusion.55, s32[384]{0:T(512)S(1)} %fusion.54), channel_id=1, replica_groups=mesh['fsdp'=4,'ctx'=4,'uly'=2] {'ctx'}, use_global_device_ids=true, to_apply=%add.2 | all-reduce | flops 1152 | bytes 9216
  57.0 0.7 broadcast_compare_fusion.2
  57.8 4.2 %fusion.6 = (f32[4,8,96]{2,1,0:T(8,128)S(1)}, f32[4,384,96,8]{1,2,3,0:T(8,128)}) fusion(pred[96,384]{1,0:T(8,128)(4,1)S(1)} %broadcast_compare_fusion.2, bf16[384,4,128,1]{0,2,3,1:T(8,128)(2,1)S(1)} %bitcast.150, bf16[96,4,8,128]{3,0,2,1:T(8,128)(2,1)} %bitcast.147), kind=kOutput, calls=%fused_computation.13 | convolution fusion | flops 305525760 | bytes 5947392 | tf_op jit(solution)/shard_map/qgrd,kgd->grqk/dot_general | solution.py:51
  62.0 14.7 %all_gather.25 = bf16[1,384,512]{2,1,0:T(8,128)(2,1)S(1)} all-gather(bf16[1,96,512]{2,1,0:T(8,128)(2,1)S(1)} %slice.126), channel_id=1, replica_groups=mesh['fsdp'=4,'ctx'=4,'uly'=2] {'ctx'}, dimensions={1}, use_global_device_ids=true | all-gather | bytes 491520 | tf_op jit(solution)/shard_map/all_gather | solution.py:166
  77.1 3.2 %fusion.3 = (f32[4,8,96]{2,1,0:T(8,128)S(1)}, f32[4,384,96,8]{1,2,3,0:T(8,128)}) fusion(pred[96,384]{1,0:T(8,128)(4,1)S(1)} %broadcast_compare_fusion.1, bf16[384,4,128,1]{0,2,3,1:T(8,128)(2,1)S(1)} %bitcast.152, bf16[96,4,8,128]{3,0,2,1:T(8,128)(2,1)S(1)} %bitcast.146), kind=kOutput, calls=%fused_computation.8 | convolution fusion | flops 305525760 | bytes 5947392 | tf_op jit(solution)/shard_map/qgrd,kgd->grqk/dot_general | solution.py:51
  80.3 15.1 %all_gather.27 = bf16[1,384,512]{2,1,0:T(8,128)(2,1)S(1)} all-gather(bf16[1,96,512]{2,1,0:T(8,128)(2,1)S(1)} %slice.132), channel_id=1, replica_groups=mesh['fsdp'=4,'ctx'=4,'uly'=2] {'ctx'}, dimensions={1}, use_global_device_ids=true | all-gather | bytes 491520 | tf_op jit(solution)/shard_map/all_gather | solution.py:166
  95.6 3.4 %fusion.9 = f32[4,8,96]{2,1,0:T(8,128)S(1)} fusion(f32[4,384,96,8]{1,2,3,0:T(8,128)} %get-tuple-element.33, f32[4,8,96]{2,1,0:T(8,128)S(1)} %broadcast_maximum_fusion.2, pred[96,384]{1,0:T(8,128)(4,1)S(1)} %broadcast_compare_fusion.2), kind=kLoop, calls=%fused_computation.19 | loop fusion | flops 4715520 | bytes 4780032 | tf_op jit(solution)/shard_map/reduce_sum | solution.py:59
  99.3 1.6 %fusion.11 = f32[4,8,96]{2,1,0:T(8,128)S(1)} fusion(f32[4,384,96,8]{1,2,3,0:T(8,128)S(1)} %copy-done.1, f32[4,8,96]{2,1,0:T(8,128)S(1)} %broadcast_maximum_fusion.1, pred[96,384]{1,0:T(8,128)(4,1)S(1)} %broadcast_compare_fusion.1), kind=kLoop, calls=%fused_computation.21 | loop fusion | flops 4715520 | bytes 4780032 | tf_op jit(solution)/shard_map/reduce_sum | solution.py:59
  101.0 1.0 fusion
  102.1 1.5 %collective-permute-start.7 = (bf16[1,96,512]{1,2,0:T(8,128)(2,1)}, bf16[1,96,512]{1,2,0:T(8,128)(2,1)S(1)}, u32[]{:S(2)}, u32[]{:S(2)}) collective-permute-start(bf16[1,96,512]{1,2,0:T(8,128)(2,1)} %bitcast.31), channel_id=1, source_target_pairs={{0,6},{2,0},{4,2},{6,4},{1,7},{3,1},{5,3},{7,5},{8,14},{10,8},{12,... | collective-permute-start | bytes 294920 | tf_op jit(solution)/shard_map/ppermute | solution.py:23
  103.7 0.5 collective-permute-start.2
  104.2 2.2 %fusion.13 = f32[4,8,96]{2,1,0:T(8,128)} fusion(f32[4,384,96,8]{1,2,3,0:T(8,128)S(1)} %get-tuple-element.29, f32[4,8,96]{2,1,0:T(8,128)S(1)} %broadcast_maximum_fusion, pred[96,384]{1,0:T(8,128)(4,1)S(1)} %broadcast_compare_fusion), kind=kLoop, calls=%fused_computation.23 | loop fusion | flops 4715520 | bytes 4780032 | tf_op jit(solution)/shard_map/reduce_sum | solution.py:59
  106.5 1.2 dynamic_update_slice.36
  107.8 1.2 dynamic_update_slice.40
  109.1 1.2 dynamic_update_slice.44
  110.3 1.6 %dynamic_update_slice.37 = bf16[1,384,512]{1,2,0:T(8,128)(2,1)S(1)} dynamic-update-slice(bf16[1,384,512]{1,2,0:T(8,128)(2,1)S(1)} %dynamic_update_slice.36, bf16[1,96,512]{1,2,0:T(8,128)(2,1)} %collective-permute-done, s32[]{:T(128)} %constant.60.clone.1, s32[]{:T(128)S(6)} %select_n.79, s32[]{:T(128)} %constant.60.clone.1) | dynamic-update-slice | bytes 196612 | tf_op jit(solution)/shard_map/dynamic_update_slice | solution.py:21
  112.0 1.6 %dynamic_update_slice.41 = bf16[1,384,512]{1,2,0:T(8,128)(2,1)S(1)} dynamic-update-slice(bf16[1,384,512]{1,2,0:T(8,128)(2,1)S(1)} %dynamic_update_slice.40, bf16[1,96,512]{1,2,0:T(8,128)(2,1)} %collective-permute-done.3, s32[]{:T(128)} %constant.60.clone.1, s32[]{:T(128)S(6)} %select_n.79, s32[]{:T(128)} %constant.60.clone.1) | dynamic-update-slice | bytes 196612 | tf_op jit(solution)/shard_map/dynamic_update_slice | solution.py:21
  113.6 0.5 collective-permute-start.5
  114.1 1.6 %dynamic_update_slice.45 = bf16[1,384,512]{1,2,0:T(8,128)(2,1)S(1)} dynamic-update-slice(bf16[1,384,512]{1,2,0:T(8,128)(2,1)S(1)} %dynamic_update_slice.44, bf16[1,96,512]{1,2,0:T(8,128)(2,1)} %collective-permute-done.6, s32[]{:T(128)} %constant.60.clone.1, s32[]{:T(128)S(6)} %select_n.79, s32[]{:T(128)} %constant.60.clone.1) | dynamic-update-slice | bytes 196612 | tf_op jit(solution)/shard_map/dynamic_update_slice | solution.py:21
  115.8 2.1 %collective-permute-start.8 = (bf16[1,96,512]{1,2,0:T(8,128)(2,1)}, bf16[1,96,512]{1,2,0:T(8,128)(2,1)}, u32[]{:S(2)}, u32[]{:S(2)}) collective-permute-start(bf16[1,96,512]{1,2,0:T(8,128)(2,1)} %collective-permute-done.6), channel_id=1, source_target_pairs={{0,2},{2,4},{4,6},{6,0},{1,3},{3,5},{5,7},{7,1},{8,10},{10,12},{12... | collective-permute-start | bytes 294920 | tf_op jit(solution)/shard_map/ppermute | solution.py:20
  117.9 1.6 %dynamic_update_slice.38 = bf16[1,384,512]{1,2,0:T(8,128)(2,1)S(1)} dynamic-update-slice(bf16[1,384,512]{1,2,0:T(8,128)(2,1)S(1)} %dynamic_update_slice.37, bf16[1,96,512]{1,2,0:T(8,128)(2,1)} %collective-permute-done.1, s32[]{:T(128)} %constant.60.clone.1, s32[]{:T(128)S(6)} %select_n.81, s32[]{:T(128)} %constant.60.clone.1) | dynamic-update-slice | bytes 196612 | tf_op jit(solution)/shard_map/dynamic_update_slice | solution.py:24
  119.5 1.7 %dynamic_update_slice.42 = bf16[1,384,512]{1,2,0:T(8,128)(2,1)S(1)} dynamic-update-slice(bf16[1,384,512]{1,2,0:T(8,128)(2,1)S(1)} %dynamic_update_slice.41, bf16[1,96,512]{1,2,0:T(8,128)(2,1)} %collective-permute-done.4, s32[]{:T(128)} %constant.60.clone.1, s32[]{:T(128)S(6)} %select_n.81, s32[]{:T(128)} %constant.60.clone.1) | dynamic-update-slice | bytes 196612 | tf_op jit(solution)/shard_map/dynamic_update_slice | solution.py:24
  121.2 0.9 dynamic_update_slice.46
  122.1 0.9 dynamic_update_slice.39
  123.1 3.7 %fusion.35 = bf16[96,4,8,128]{3,0,2,1:T(8,128)(2,1)S(1)} fusion(bf16[384,4,128,1]{0,2,3,1:T(8,128)(2,1)S(1)} %bitcast.154, f32[4,384,96,8]{1,2,3,0:T(8,128)} %get-tuple-element.33, f32[4,8,96]{2,1,0:T(8,128)S(1)} %broadcast_maximum_fusion.2, pred[96,384]{1,0:T(8,128)(4,1)S(1)} %broadcast_compare_fusion.2, f32[96,4,8]{0,2,1:T(8,128)S(1)} %bitcast.160), kind=kOutput, calls=%fused_computation.50 | convolution fusion | flops 307494912 | bytes 5959680 | tf_op jit(solution)/shard_map/grqk,kgd->grqd/dot_general | solution.py:60
  126.8 0.9 dynamic_update_slice.43
  127.7 3.7 %fusion.34 = bf16[96,4,8,128]{3,0,2,1:T(8,128)(2,1)S(1)} fusion(bf16[384,4,128,1]{0,2,3,1:T(8,128)(2,1)S(1)} %bitcast.155, f32[4,384,96,8]{1,2,3,0:T(8,128)} %get-tuple-element.31, f32[4,8,96]{2,1,0:T(8,128)S(1)} %broadcast_maximum_fusion.1, pred[96,384]{1,0:T(8,128)(4,1)S(1)} %broadcast_compare_fusion.1, f32[96,4,8]{0,2,1:T(8,128)S(1)} %bitcast.158), kind=kOutput, calls=%fused_computation.48 | convolution fusion | flops 307494912 | bytes 5959680 | tf_op jit(solution)/shard_map/grqk,kgd->grqd/dot_general | solution.py:60
  132.7 1.7 %dynamic_update_slice.47 = bf16[1,384,512]{1,2,0:T(8,128)(2,1)S(1)} dynamic-update-slice(bf16[1,384,512]{1,2,0:T(8,128)(2,1)S(1)} %dynamic_update_slice.46, bf16[1,96,512]{1,2,0:T(8,128)(2,1)} %collective-permute-done.8, s32[]{:T(128)} %constant.60.clone.1, s32[]{:T(128)S(6)} %select_n.83, s32[]{:T(128)} %constant.60.clone.1) | dynamic-update-slice | bytes 196612 | tf_op jit(solution)/shard_map/dynamic_update_slice | solution.py:21
  134.4 3.7 %fusion.33 = bf16[96,4,8,128]{3,0,2,1:T(8,128)(2,1)S(1)} fusion(bf16[384,4,128,1]{0,2,3,1:T(8,128)(2,1)S(1)} %bitcast.153, f32[4,384,96,8]{1,2,3,0:T(8,128)} %copy-done.2, f32[4,8,96]{2,1,0:T(8,128)} %copy-done.11, pred[96,384]{1,0:T(8,128)(4,1)} %copy-done.10, f32[96,4,8]{0,2,1:T(8,128)} %bitcast.159), kind=kOutput, calls=%fused_computation.46 | convolution fusion | flops 307494912 | bytes 5959680 | tf_op jit(solution)/shard_map/grqk,kgd->grqd/dot_general | solution.py:60
  138.7 1.7 %pad_maximum_fusion = bf16[3,96,4096]{2,1,0:T(8,128)(2,1)} fusion(bf16[1,96,4096]{2,1,0:T(8,128)(2,1)S(1)} %convert_element_type.78, bf16[1,96,4096]{2,1,0:T(8,128)(2,1)S(1)} %convert_element_type.75, bf16[1,96,4096]{2,1,0:T(8,128)(2,1)S(1)} %convert_element_type.72), kind=kLoop, calls=%fused_computation.28 | loop fusion | flops 2359296 | bytes 4718592 | tf_op jit(solution)/shard_map/concatenate | solution.py:173
  (81 shorter events, 4.6 us)
Async XLA Ops:
  0.0 20.3 %copy-start = (f32[2,64]{1,0:T(2,128)S(1)}, f32[2,64]{1,0:T(2,128)}, u32[]{:S(2)}) copy-start(f32[2,64]{1,0:T(2,128)} %param.12) | copy-start | bytes 1540
  0.0 20.3 %copy-start.15 = (s32[3]{0:T(128)S(1)}, s32[3]{0:T(128)}, u32[]{:S(2)}) copy-start(s32[3]{0:T(128)} %param.13) | copy-start | bytes 40
  8.1 30.1 %copy-start.4 = (bf16[3,96,4096]{2,1,0:T(8,128)(2,1)S(1)}, bf16[3,96,4096]{2,1,0:T(8,128)(2,1)}, u32[]{:S(2)}) copy-start(bf16[3,96,4096]{2,1,0:T(8,128)(2,1)} %param.7) | copy-start | bytes 7077892
  9.1 93.0 %collective-permute-start = (bf16[1,96,512]{1,2,0:T(8,128)(2,1)}, bf16[1,96,512]{1,2,0:T(8,128)(2,1)}, u32[]{:S(2)}, u32[]{:S(2)}) collective-permute-start(bf16[1,96,512]{1,2,0:T(8,128)(2,1)} %bitcast.11), channel_id=1, source_target_pairs={{0,2},{2,4},{4,6},{6,0},{1,3},{3,5},{5,7},{7,1},{8,10},{10,12},{12... | collective-permute-start | bytes 294920 | tf_op jit(solution)/shard_map/ppermute | solution.py:20
  11.1 104.6 %collective-permute-start.1 = (bf16[1,96,512]{1,2,0:T(8,128)(2,1)}, bf16[1,96,512]{1,2,0:T(8,128)(2,1)}, u32[]{:S(2)}, u32[]{:S(2)}) collective-permute-start(bf16[1,96,512]{1,2,0:T(8,128)(2,1)} %bitcast.11), channel_id=1, source_target_pairs={{0,6},{2,0},{4,2},{6,4},{1,7},{3,1},{5,3},{7,5},{8,14},{10,8},{12,... | collective-permute-start | bytes 294920 | tf_op jit(solution)/shard_map/ppermute | solution.py:23
  13.2 90.5 %collective-permute-start.3 = (bf16[1,96,512]{1,2,0:T(8,128)(2,1)}, bf16[1,96,512]{1,2,0:T(8,128)(2,1)}, u32[]{:S(2)}, u32[]{:S(2)}) collective-permute-start(bf16[1,96,512]{1,2,0:T(8,128)(2,1)} %bitcast.21), channel_id=1, source_target_pairs={{0,2},{2,4},{4,6},{6,0},{1,3},{3,5},{5,7},{7,1},{8,10},{10,12},{12... | collective-permute-start | bytes 294920 | tf_op jit(solution)/shard_map/ppermute | solution.py:20
  13.2 106.4 %collective-permute-start.4 = (bf16[1,96,512]{1,2,0:T(8,128)(2,1)}, bf16[1,96,512]{1,2,0:T(8,128)(2,1)}, u32[]{:S(2)}, u32[]{:S(2)}) collective-permute-start(bf16[1,96,512]{1,2,0:T(8,128)(2,1)} %bitcast.21), channel_id=1, source_target_pairs={{0,6},{2,0},{4,2},{6,4},{1,7},{3,1},{5,3},{7,5},{8,14},{10,8},{12,... | collective-permute-start | bytes 294920 | tf_op jit(solution)/shard_map/ppermute | solution.py:23
  17.0 96.6 %collective-permute-start.6 = (bf16[1,96,512]{1,2,0:T(8,128)(2,1)}, bf16[1,96,512]{1,2,0:T(8,128)(2,1)}, u32[]{:S(2)}, u32[]{:S(2)}) collective-permute-start(bf16[1,96,512]{1,2,0:T(8,128)(2,1)} %bitcast.31), channel_id=1, source_target_pairs={{0,2},{2,4},{4,6},{6,0},{1,3},{3,5},{5,7},{7,1},{8,10},{10,12},{12... | collective-permute-start | bytes 294920 | tf_op jit(solution)/shard_map/ppermute | solution.py:20
  21.1 0.7 copy-start.5
  21.1 0.7 copy-start.6
  38.2 0.9 copy-start.7
  39.1 3.6 %copy-start.16 = (u32[32]{0:T(128)S(1)}, u32[32]{0:T(128)}, u32[]{:S(2)}) copy-start(u32[32]{0:T(128)} %constant.86) | copy-start | bytes 388
  39.1 5.0 %copy-start.12 = (s32[3,96]{1,0:T(4,128)S(1)}, s32[3,96]{1,0:T(4,128)}, u32[]{:S(2)}) copy-start(s32[3,96]{1,0:T(4,128)} %param.11) | copy-start | bytes 3460
  48.5 13.5 %copy-start.9 = (bf16[1,96,4,128]{3,2,1,0:T(4,128)(2,1)S(1)}, bf16[1,96,4,128]{3,2,1,0:T(4,128)(2,1)}, u32[]{:S(2)}) copy-start(bf16[1,96,4,128]{3,2,1,0:T(4,128)(2,1)} %get-tuple-element.17) | copy-start | bytes 294916
  48.5 28.5 %copy-start.14 = (s32[96]{0:T(128)S(1)}, s32[96]{0:T(128)}, u32[]{:S(2)}) copy-start(s32[96]{0:T(128)} %get-tuple-element.27) | copy-start | bytes 1156
  48.5 28.6 %copy-start.3 = (bf16[1,96,32,128]{3,1,2,0:T(8,128)(2,1)S(1)}, bf16[1,96,32,128]{3,1,2,0:T(8,128)(2,1)}, u32[]{:S(2)}) copy-start(bf16[1,96,32,128]{3,1,2,0:T(8,128)(2,1)} %get-tuple-element.12) | copy-start | bytes 2359300
  61.9 18.3 %copy-start.8 = (bf16[1,96,4,128]{3,2,1,0:T(4,128)(2,1)S(1)}, bf16[1,96,4,128]{3,2,1,0:T(4,128)(2,1)}, u32[]{:S(2)}) copy-start(bf16[1,96,4,128]{3,2,1,0:T(4,128)(2,1)} %get-tuple-element.16) | copy-start | bytes 294916
  95.6 3.8 %copy-start.1 = (f32[4,384,96,8]{1,2,3,0:T(8,128)S(1)}, f32[4,384,96,8]{1,2,3,0:T(8,128)}, u32[]{:S(2)}) copy-start(f32[4,384,96,8]{1,2,3,0:T(8,128)} %get-tuple-element.31) | copy-start | bytes 14155780
  95.6 5.3 %copy-start.13 = (s32[96]{0:T(128)S(1)}, s32[96]{0:T(128)}, u32[]{:S(2)}) copy-start(s32[96]{0:T(128)} %get-tuple-element.26) | copy-start | bytes 1156
  101.0 5.4 %copy-start.10 = (pred[96,384]{1,0:T(8,128)(4,1)}, pred[96,384]{1,0:T(8,128)(4,1)S(1)}, u32[]{:S(2)}) copy-start(pred[96,384]{1,0:T(8,128)(4,1)S(1)} %broadcast_compare_fusion) | copy-start | bytes 110596
  102.1 2.2 %copy-start.2 = (f32[4,384,96,8]{1,2,3,0:T(8,128)}, f32[4,384,96,8]{1,2,3,0:T(8,128)S(1)}, u32[]{:S(2)}) copy-start(f32[4,384,96,8]{1,2,3,0:T(8,128)S(1)} %get-tuple-element.29) | copy-start | bytes 14155780
  102.1 11.5 %copy-start.11 = (f32[4,8,96]{2,1,0:T(8,128)}, f32[4,8,96]{2,1,0:T(8,128)S(1)}, u32[]{:S(2)}) copy-start(f32[4,8,96]{2,1,0:T(8,128)S(1)} %broadcast_maximum_fusion) | copy-start | bytes 36868
  102.1 19.1 %collective-permute-start.7 = (bf16[1,96,512]{1,2,0:T(8,128)(2,1)}, bf16[1,96,512]{1,2,0:T(8,128)(2,1)S(1)}, u32[]{:S(2)}, u32[]{:S(2)}) collective-permute-start(bf16[1,96,512]{1,2,0:T(8,128)(2,1)} %bitcast.31), channel_id=1, source_target_pairs={{0,6},{2,0},{4,2},{6,4},{1,7},{3,1},{5,3},{7,5},{8,14},{10,8},{12,... | collective-permute-start | bytes 294920 | tf_op jit(solution)/shard_map/ppermute | solution.py:23
  103.7 18.5 %collective-permute-start.2 = (bf16[1,96,512]{1,2,0:T(8,128)(2,1)}, bf16[1,96,512]{1,2,0:T(8,128)(2,1)S(1)}, u32[]{:S(2)}, u32[]{:S(2)}) collective-permute-start(bf16[1,96,512]{1,2,0:T(8,128)(2,1)} %collective-permute-done), channel_id=1, source_target_pairs={{0,2},{2,4},{4,6},{6,0},{1,3},{3,5},{5,7},{7,1},{8,10},{10,12},{12... | collective-permute-start | bytes 294920 | tf_op jit(solution)/shard_map/ppermute | solution.py:20
  113.6 13.2 %collective-permute-start.5 = (bf16[1,96,512]{1,2,0:T(8,128)(2,1)}, bf16[1,96,512]{1,2,0:T(8,128)(2,1)S(1)}, u32[]{:S(2)}, u32[]{:S(2)}) collective-permute-start(bf16[1,96,512]{1,2,0:T(8,128)(2,1)} %collective-permute-done.3), channel_id=1, source_target_pairs={{0,2},{2,4},{4,6},{6,0},{1,3},{3,5},{5,7},{7,1},{8,10},{10,12},{12... | collective-permute-start | bytes 294920 | tf_op jit(solution)/shard_map/ppermute | solution.py:20
  115.8 16.9 %collective-permute-start.8 = (bf16[1,96,512]{1,2,0:T(8,128)(2,1)}, bf16[1,96,512]{1,2,0:T(8,128)(2,1)}, u32[]{:S(2)}, u32[]{:S(2)}) collective-permute-start(bf16[1,96,512]{1,2,0:T(8,128)(2,1)} %collective-permute-done.6), channel_id=1, source_target_pairs={{0,2},{2,4},{4,6},{6,0},{1,3},{3,5},{5,7},{7,1},{8,10},{10,12},{12... | collective-permute-start | bytes 294920 | tf_op jit(solution)/shard_map/ppermute | solution.py:20
